TPU v7x, 32 devices: a whole 2x2x4 slice. The times are simulated.
32 devices in a mesh: pipe: 2 (over x), fsdp: 8 (over z, y), tp: 2 (over core).
Axes of the slice: x: 2, y: 2, z: 4, core: 2. Of those that a mesh axis runs over, the one named last changes fastest.
Arguments:
- inputs: bfloat16 [4, 512, 1152], P(None, ('fsdp', 'tp')), may hold values from -6 to 6
- cotangent: bfloat16 [4, 512, 1152], P(None, ('fsdp', 'tp')), may hold values from -6 to 6
- image_ids: int32 [4, 512], replicated, may hold values from 0 to 2, as said below
- proj_in: bfloat16 [2, 1152, 3, 1152], P('pipe', 'fsdp', None, 'tp'), may hold values from -0.1875 to 0.1875
- bias_in: bfloat16 [2, 2, 1152], P('pipe', None, 'tp'), may hold values from -3 to 3
- proj_out: bfloat16 [2, 1152, 1152], P('pipe', 'fsdp', 'tp'), may hold values from -3 to 3
- bias_out: bfloat16 [2, 1152], P('pipe'), may hold values from -3 to 3
- gain_attn: bfloat16 [2, 1152], P('pipe'), may hold values from 0.25 to 1.75
- shift_attn: bfloat16 [2, 1152], P('pipe'), may hold values from -2 to 2
- up_projection: bfloat16 [2, 1152, 4304], P('pipe', 'fsdp', 'tp'), may hold values from -0.1875 to 0.1875
- up_bias_vector: bfloat16 [2, 4304], P('pipe', 'tp'), may hold values from -3 to 3
- down_projection: bfloat16 [2, 1152, 4304], P('pipe', 'fsdp', 'tp'), may hold values from -0.09375 to 0.09375
- bias_down: bfloat16 [2, 1152], P('pipe'), may hold values from -3 to 3
- gain_feed: bfloat16 [2, 1152], P('pipe'), may hold values from 0.25 to 1.75
- shift_feed: bfloat16 [2, 1152], P('pipe'), may hold values from -2 to 2
Outputs:
- activations: bfloat16 [2, 4, 512, 1152], P('pipe', None, ('fsdp', 'tp'))
- grad_inputs: bfloat16 [2, 4, 512, 1152], P('pipe', None, ('fsdp', 'tp'))
- grad_proj_in: float32 [2, 1152, 3, 1152], P('pipe', 'fsdp', None, 'tp')
- grad_bias_in: float32 [2, 2, 1152], P('pipe', None, 'tp')
- grad_proj_out: float32 [2, 1152, 1152], P('pipe', 'fsdp', 'tp')
- grad_bias_out: float32 [2, 1152], P('pipe')
- grad_gain_attn: float32 [2, 1152], P('pipe')
- grad_shift_attn: float32 [2, 1152], P('pipe')
- grad_proj_up: float32 [2, 1152, 4304], P('pipe', 'fsdp', 'tp')
- grad_bias_up: float32 [2, 4304], P('pipe', 'tp')
- grad_proj_down: float32 [2, 1152, 4304], P('pipe', 'fsdp', 'tp')
- grad_bias_down: float32 [2, 1152], P('pipe')
- grad_gain_feed: float32 [2, 1152], P('pipe')
- grad_shift_feed: float32 [2, 1152], P('pipe')
Inputs may be any that keep to these rules, and one draw needn't show every extreme that they name: `image_ids`: every image has 1 to 256 rows of its micro-batch, and one has exactly 256.
All inputs are finite; a program needn't handle non-finite values.
Results may differ from a plain program's by a relative error of at most 0.014.
Values may be sent and summed in bfloat16 or wider, within the bound.
No kernel may reach another device: no remote copies, remote signals or barrier semaphores. Data moves between devices by JAX's collectives and lax.ppermute only.
A program may use at most 256 MiB of HBM per device.

v0:
```python
import jax
import jax.numpy as jnp
from jax import lax
from jax.sharding import PartitionSpec as P

HD = 72


EPSILON = 1e-06
MASKED = -1e30


def from_behind(value, axis, steps):
    count = lax.axis_size(axis)
    initial, last = (max(0, -steps), min(count, count - steps))
    return lax.ppermute(value, axis, [(source, source + steps) for source in range(initial, last)])


def normalize(values, gain_vec, shift_vec):
    row_mean = jnp.mean(values, axis=-1, keepdims=True)
    center = values - row_mean
    spread = jnp.mean(center * center, axis=-1, keepdims=True)
    return center * lax.rsqrt(spread + EPSILON) * gain_vec + shift_vec


def gelu_tanh(values):
    return jax.nn.gelu(values, approximate=True)


def rows_gather(values):
    return lax.all_gather(values, "tp", axis=0, tiled=True)


def rows_reduce(values):
    return lax.psum_scatter(values, "tp", scatter_dimension=0, tiled=True)


def grad_gather(values):
    return lax.all_gather(values, "tp", axis=0, tiled=True)


def grad_reduce(values):
    return lax.psum_scatter(values, "tp", scatter_dimension=0, tiled=True)


def contract_last(left, right):
    return lax.dot_general(
        left, right, (((1,), (1,)), ((), ())), preferred_element_type=jnp.float32
    )


def head_scores(query_low, keys_all, same_image, heads_local):
    query_h = query_low.reshape(query_low.shape[0], heads_local, HD)
    keys_h = keys_all.reshape(keys_all.shape[0], heads_local, HD)
    raw_scores = jnp.einsum(
        "qhe,khe->hqk", query_h, keys_h, preferred_element_type=jnp.float32
    ) * HD ** (-0.5)
    return jnp.where(same_image[None], raw_scores, MASKED)


def put_slot(buffer, value, slot_num):
    return lax.dynamic_update_index_in_dim(buffer, value, slot_num, 0)


def get_slot(buffer, slot_num):
    return lax.dynamic_index_in_dim(buffer, slot_num, 0, keepdims=False)


def body(
    inputs,
    cotangent,
    image_ids,
    proj_in,
    bias_in,
    proj_out,
    bias_out,
    gain_attn,
    shift_attn,
    up_projection,
    up_bias_vector,
    down_projection,
    bias_down,
    gain_feed,
    shift_feed,
):
    micro_count = inputs.shape[0]
    half_rows = inputs.shape[1]
    model_width = inputs.shape[2]
    local_cols = proj_in.shape[3]
    heads_local = local_cols // HD
    hidden_cols = up_projection.shape[2]
    section_num = lax.axis_index("pipe")
    block_num = lax.axis_index("fsdp")
    tok_rows = half_rows * lax.axis_size("tp")
    all_rows = tok_rows * lax.axis_size("fsdp")
    slot_count = micro_count + 1
    score_scale = HD ** (-0.5)
    weight_in, weight_out, weight_up, weight_down = (
        lax.all_gather(proj_in[0], "fsdp", axis=0, tiled=True),
        lax.all_gather(proj_out[0], "fsdp", axis=0, tiled=True),
        lax.all_gather(up_projection[0], "fsdp", axis=0, tiled=True),
        lax.all_gather(down_projection[0], "fsdp", axis=0, tiled=True),
    )
    qv_bias = bias_in[0].astype(jnp.float32)
    out_shift = bias_out[0].astype(jnp.float32)
    attn_gain = gain_attn[0].astype(jnp.float32)
    attn_shift = shift_attn[0].astype(jnp.float32)
    up_shift = up_bias_vector[0].astype(jnp.float32)
    down_shift = bias_down[0].astype(jnp.float32)
    feed_gain = gain_feed[0].astype(jnp.float32)
    feed_shift = shift_feed[0].astype(jnp.float32)
    keep_input = jnp.zeros((slot_count, half_rows, model_width), jnp.float32)
    keep_middle = jnp.zeros((slot_count, half_rows, model_width), jnp.float32)
    keep_normed = jnp.zeros((slot_count, tok_rows, model_width), jnp.bfloat16)
    keep_query = jnp.zeros((slot_count, tok_rows, local_cols), jnp.bfloat16)
    keep_keys = jnp.zeros((slot_count, all_rows, local_cols), jnp.bfloat16)
    keep_values = jnp.zeros((slot_count, all_rows, local_cols), jnp.bfloat16)
    keep_lse = jnp.zeros((slot_count, heads_local, tok_rows), jnp.float32)
    keep_context = jnp.zeros((slot_count, tok_rows, local_cols), jnp.bfloat16)
    keep_feed = jnp.zeros((slot_count, tok_rows, model_width), jnp.bfloat16)
    keep_hidden = jnp.zeros((slot_count, tok_rows, hidden_cols), jnp.float32)
    act_store = jnp.zeros((slot_count, half_rows, model_width), jnp.bfloat16)
    received = jnp.zeros((half_rows, model_width), jnp.bfloat16)
    for step_num in range(micro_count + 1):
        index_mb = step_num - section_num
        slot_num = (index_mb + slot_count) % slot_count
        take_num = jnp.clip(index_mb, 0, micro_count - 1)
        fresh_rows = get_slot(inputs, take_num)
        rows_now = jnp.where(section_num == 0, fresh_rows, received).astype(jnp.float32)
        batch_ids = get_slot(image_ids, take_num)
        query_ids = lax.dynamic_slice_in_dim(batch_ids, block_num * tok_rows, tok_rows)
        same_image = query_ids[:, None] == batch_ids[None, :]
        normed = rows_gather(normalize(rows_now, attn_gain, attn_shift).astype(jnp.bfloat16))
        projected = jnp.einsum("rd,dce->rce", normed, weight_in, preferred_element_type=jnp.float32)
        query_low = (projected[:, 0] + qv_bias[0]).astype(jnp.bfloat16)
        keys_own = projected[:, 1].astype(jnp.bfloat16)
        values_own = (projected[:, 2] + qv_bias[1]).astype(jnp.bfloat16)
        keys_all, values_all = (
            lax.all_gather(keys_own, "fsdp", axis=0, tiled=True),
            lax.all_gather(values_own, "fsdp", axis=0, tiled=True),
        )
        scores = head_scores(query_low, keys_all, same_image, heads_local)
        row_max = jnp.max(scores, axis=-1, keepdims=True)
        exp_scores = jnp.exp(scores - row_max)
        row_total = jnp.sum(exp_scores, axis=-1, keepdims=True)
        soft_probs = (exp_scores / row_total).astype(jnp.bfloat16)
        log_total = (row_max + jnp.log(row_total))[:, :, 0]
        context = jnp.einsum(
            "hqk,khe->qhe",
            soft_probs,
            values_all.reshape(all_rows, heads_local, HD),
            preferred_element_type=jnp.float32,
        )
        context = context.reshape(tok_rows, local_cols).astype(jnp.bfloat16)
        middle = rows_now + rows_reduce(contract_last(context, weight_out)) + out_shift
        feed_input = rows_gather(normalize(middle, feed_gain, feed_shift).astype(jnp.bfloat16))
        hidden_state = jnp.dot(feed_input, weight_up, preferred_element_type=jnp.float32) + up_shift
        active_section = gelu_tanh(hidden_state).astype(jnp.bfloat16)
        result = middle + rows_reduce(contract_last(active_section, weight_down)) + down_shift
        result_low = result.astype(jnp.bfloat16)
        keep_input = put_slot(keep_input, rows_now, slot_num)
        keep_middle = put_slot(keep_middle, middle, slot_num)
        keep_normed = put_slot(keep_normed, normed, slot_num)
        keep_query = put_slot(keep_query, query_low, slot_num)
        keep_keys = put_slot(keep_keys, keys_all, slot_num)
        keep_values = put_slot(keep_values, values_all, slot_num)
        keep_lse = put_slot(keep_lse, log_total, slot_num)
        keep_context = put_slot(keep_context, context, slot_num)
        keep_feed = put_slot(keep_feed, feed_input, slot_num)
        keep_hidden = put_slot(keep_hidden, hidden_state, slot_num)
        act_store = put_slot(act_store, result_low, slot_num)
        if step_num < micro_count:
            received = from_behind(result_low, "pipe", 1)
    totals = (
        jnp.zeros(weight_in.shape, jnp.float32),
        jnp.zeros(weight_out.shape, jnp.float32),
        jnp.zeros(weight_up.shape, jnp.float32),
        jnp.zeros(weight_down.shape, jnp.float32),
    )
    qv_total = jnp.zeros((2, local_cols), jnp.float32)
    up_total = jnp.zeros((hidden_cols,), jnp.float32)
    vector_totals = tuple((jnp.zeros((model_width,), jnp.float32) for index_vec in range(6)))
    grad_store = jnp.zeros((slot_count, half_rows, model_width), jnp.bfloat16)
    incoming = jnp.zeros((half_rows, model_width), jnp.bfloat16)
    for step_num in range(micro_count + 1):
        index_mb = step_num - 1 + section_num
        valid_mask = jnp.logical_and(index_mb >= 0, index_mb < micro_count).astype(jnp.float32)
        slot_num = (index_mb + slot_count) % slot_count
        take_num = jnp.clip(index_mb, 0, micro_count - 1)
        given = get_slot(cotangent, take_num)
        grad_out = jnp.where(section_num == 1, given, incoming).astype(jnp.float32)
        batch_ids = get_slot(image_ids, take_num)
        query_ids = lax.dynamic_slice_in_dim(batch_ids, block_num * tok_rows, tok_rows)
        same_image = query_ids[:, None] == batch_ids[None, :]
        rows_now = get_slot(keep_input, slot_num)
        middle = get_slot(keep_middle, slot_num)
        normed = get_slot(keep_normed, slot_num)
        query_low = get_slot(keep_query, slot_num)
        log_total = get_slot(keep_lse, slot_num)
        context = get_slot(keep_context, slot_num)
        feed_input = get_slot(keep_feed, slot_num)
        hidden_state = get_slot(keep_hidden, slot_num)
        keys_all = get_slot(keep_keys, slot_num)
        values_all = get_slot(keep_values, slot_num)
        down_grad = grad_gather(grad_out.astype(jnp.bfloat16))
        active_section = gelu_tanh(hidden_state).astype(jnp.bfloat16)
        grad_down_w = jnp.einsum(
            "rd,rf->df", down_grad, active_section, preferred_element_type=jnp.float32
        )
        active_grad = jnp.dot(down_grad, weight_down, preferred_element_type=jnp.float32)
        gelu_value, gelu_back = jax.vjp(gelu_tanh, hidden_state)
        hidden_grad = gelu_back(active_grad)[0].astype(jnp.bfloat16)
        grad_up_w = jnp.einsum(
            "rd,rf->df", feed_input, hidden_grad, preferred_element_type=jnp.float32
        )
        feed_grad = grad_reduce(contract_last(hidden_grad, weight_up))
        feed_value, feed_back = jax.vjp(normalize, middle, feed_gain, feed_shift)
        middle_part, feed_gain_grad, feed_shift_grad = feed_back(feed_grad)
        middle_grad = grad_out + middle_part
        attn_grad = grad_gather(middle_grad.astype(jnp.bfloat16))
        grad_out_w = jnp.einsum("rd,rj->dj", attn_grad, context, preferred_element_type=jnp.float32)
        context_grad = jnp.dot(attn_grad, weight_out, preferred_element_type=jnp.float32).astype(
            jnp.bfloat16
        )
        scores = head_scores(query_low, keys_all, same_image, heads_local)
        soft_probs = jnp.exp(scores - log_total[:, :, None])
        context_h = context_grad.reshape(tok_rows, heads_local, HD)
        values_h = values_all.reshape(all_rows, heads_local, HD)
        keys_h = keys_all.reshape(all_rows, heads_local, HD)
        query_h = query_low.reshape(tok_rows, heads_local, HD)
        prob_grad = jnp.einsum(
            "qhe,khe->hqk", context_h, values_h, preferred_element_type=jnp.float32
        )
        inner = jnp.sum(soft_probs * prob_grad, axis=-1, keepdims=True)
        score_grad = (soft_probs * (prob_grad - inner)).astype(jnp.bfloat16)
        query_grad = (
            jnp.einsum("hqk,khe->qhe", score_grad, keys_h, preferred_element_type=jnp.float32)
            * score_scale
        )
        query_grad = query_grad.reshape(tok_rows, local_cols).astype(jnp.bfloat16)
        key_part = (
            jnp.einsum("hqk,qhe->khe", score_grad, query_h, preferred_element_type=jnp.float32)
            * score_scale
        ).reshape(all_rows, local_cols)
        value_part = jnp.einsum(
            "hqk,qhe->khe",
            soft_probs.astype(jnp.bfloat16),
            context_h,
            preferred_element_type=jnp.float32,
        ).reshape(all_rows, local_cols)
        key_sum, value_sum = (
            lax.psum_scatter(key_part, "fsdp", scatter_dimension=0, tiled=True),
            lax.psum_scatter(value_part, "fsdp", scatter_dimension=0, tiled=True),
        )
        key_grad = key_sum.astype(jnp.bfloat16)
        value_grad = value_sum.astype(jnp.bfloat16)
        joined = jnp.stack((query_grad, key_grad, value_grad), axis=1)
        grad_in_w = jnp.einsum("rd,rce->dce", normed, joined, preferred_element_type=jnp.float32)
        normed_grad = grad_reduce(
            jnp.einsum("rce,dce->rd", joined, weight_in, preferred_element_type=jnp.float32)
        )
        attn_value, attn_back = jax.vjp(normalize, rows_now, attn_gain, attn_shift)
        rows_part, attn_gain_grad, attn_shift_grad = attn_back(normed_grad)
        input_grad = (middle_grad + rows_part).astype(jnp.bfloat16)
        grad_store = put_slot(grad_store, input_grad, slot_num)
        qv_step = jnp.stack(
            (
                jnp.sum(query_grad.astype(jnp.float32), axis=0),
                jnp.sum(value_grad.astype(jnp.float32), axis=0),
            )
        )
        qv_total = qv_total + valid_mask * qv_step
        up_total = up_total + valid_mask * jnp.sum(hidden_grad.astype(jnp.float32), axis=0)
        vector_steps = (
            jnp.sum(middle_grad, axis=0),
            attn_gain_grad,
            attn_shift_grad,
            jnp.sum(grad_out, axis=0),
            feed_gain_grad,
            feed_shift_grad,
        )
        vector_totals = tuple(
            (
                old_vec + valid_mask * new_vec
                for old_vec, new_vec in zip(vector_totals, vector_steps)
            )
        )
        step_in = valid_mask * grad_in_w
        step_out = valid_mask * grad_out_w
        step_up = valid_mask * grad_up_w
        step_down = valid_mask * grad_down_w
        totals = (
            totals[0] + step_in,
            totals[1] + step_out,
            totals[2] + step_up,
            totals[3] + step_down,
        )
        if step_num < micro_count:
            incoming = from_behind(input_grad, "pipe", -1)
    totals = (
        lax.psum_scatter(totals[0], "fsdp", scatter_dimension=0, tiled=True),
        lax.psum_scatter(totals[1], "fsdp", scatter_dimension=0, tiled=True),
        lax.psum_scatter(totals[2], "fsdp", scatter_dimension=0, tiled=True),
        lax.psum_scatter(totals[3], "fsdp", scatter_dimension=0, tiled=True),
    )
    qv_sum, up_sum = lax.psum((qv_total, up_total), "fsdp")
    vector_sums = lax.psum(
        (
            vector_totals[0],
            vector_totals[1],
            vector_totals[2],
            vector_totals[3],
            vector_totals[4],
            vector_totals[5],
        ),
        ("fsdp", "tp"),
    )
    return (
        act_store[:micro_count][None],
        grad_store[:micro_count][None],
        totals[0][None],
        qv_sum[None],
        totals[1][None],
        vector_sums[0][None],
        vector_sums[1][None],
        vector_sums[2][None],
        totals[2][None],
        up_sum[None],
        totals[3][None],
        vector_sums[3][None],
        vector_sums[4][None],
        vector_sums[5][None],
    )


def solution(mesh):
    placed = (
        P(None, ("fsdp", "tp"), None),
        P(None, ("fsdp", "tp"), None),
        P(),
        P("pipe", "fsdp", None, "tp"),
        P("pipe", None, "tp"),
        P("pipe", "fsdp", "tp"),
        P("pipe", None),
        P("pipe", None),
        P("pipe", None),
        P("pipe", "fsdp", "tp"),
        P("pipe", "tp"),
        P("pipe", "fsdp", "tp"),
        P("pipe", None),
        P("pipe", None),
        P("pipe", None),
    )
    return jax.shard_map(
        body,
        mesh=mesh,
        in_specs=placed,
        out_specs=(
            P("pipe", None, ("fsdp", "tp"), None),
            P("pipe", None, ("fsdp", "tp"), None),
            P("pipe", "fsdp", None, "tp"),
            P("pipe", None, "tp"),
            P("pipe", "fsdp", "tp"),
            P("pipe", None),
            P("pipe", None),
            P("pipe", None),
            P("pipe", "fsdp", "tp"),
            P("pipe", "tp"),
            P("pipe", "fsdp", "tp"),
            P("pipe", None),
            P("pipe", None),
            P("pipe", None),
        ),
        check_vma=False,
    )
```

profile of v0, /device:TPU:0, one launch (start us, length us, event | category | flops | bytes accessed | tf_op | source)
XLA Modules:
  0.0 2377.8 jit_solution(1234616215438698280)
XLA Ops:
  19.7 68.9 %all-gather.15.cloned.1.call-done = bf16[1,1152,3,576]{3,1,2,0:T(8,128)(2,1)} async-done(((bf16[1,144,3,576]{3,1,2,0:T(8,128)(2,1)}), bf16[1,1152,3,576]{3,1,2,0:T(8,128)(2,1)}) %all-gather.15.cloned.1.call-update) | async-done | bytes 3981328 | tf_op jit(solution)/shard_map/all_gather | solution.py:99
  174.3 82.8 %all-gather.19.cloned.1.call-done = bf16[1,1152,2152]{2,1,0:T(8,128)(2,1)} async-done(((bf16[1,144,2152]{2,1,0:T(8,128)(2,1)}), bf16[1,1152,2152]{2,1,0:T(8,128)(2,1)}) %all-gather.19.cloned.1.call-update) | async-done | bytes 4958224 | tf_op jit(solution)/shard_map/all_gather | solution.py:101
  263.1 77.3 %all-gather.21.cloned.1.call-done = bf16[1,1152,2152]{2,1,0:T(8,128)(2,1)} async-done(((bf16[1,144,2152]{2,1,0:T(8,128)(2,1)}), bf16[1,1152,2152]{2,1,0:T(8,128)(2,1)}) %all-gather.21.cloned.1.call-update) | async-done | bytes 4958224 | tf_op jit(solution)/shard_map/all_gather | solution.py:102
  483.0 33.9 %all_gather.115 = bf16[512,576]{1,0:T(8,128)(2,1)} all-gather(bf16[64,576]{1,0:T(8,128)(2,1)} %fusion.354), channel_id=1, replica_groups=mesh['pipe'=2,'fsdp'=8,'tp'=2] {'fsdp'}, dimensions={0}, use_global_device_ids=true | all-gather | bytes 663552 | tf_op jit(solution)/shard_map/all_gather | solution.py:140
  516.8 33.9 %all-gather.6 = bf16[512,1,576]{2,0,1:T(8,128)(2,1)} all-gather(bf16[64,1,576]{2,0,1:T(8,128)(2,1)} %slice.151), channel_id=8, replica_groups=mesh['pipe'=2,'fsdp'=8,'tp'=2] {'fsdp'}, dimensions={0}, use_global_device_ids=true | all-gather | bytes 663552 | tf_op jit(solution)/shard_map/all_gather | solution.py:139
  608.0 34.0 %all_gather.119 = bf16[512,576]{1,0:T(8,128)(2,1)} all-gather(bf16[64,576]{1,0:T(8,128)(2,1)} %fusion.352), channel_id=1, replica_groups=mesh['pipe'=2,'fsdp'=8,'tp'=2] {'fsdp'}, dimensions={0}, use_global_device_ids=true | all-gather | bytes 663552 | tf_op jit(solution)/shard_map/all_gather | solution.py:140
  642.0 33.9 %all-gather.7 = bf16[512,1,576]{2,0,1:T(8,128)(2,1)} all-gather(bf16[64,1,576]{2,0,1:T(8,128)(2,1)} %slice.150), channel_id=9, replica_groups=mesh['pipe'=2,'fsdp'=8,'tp'=2] {'fsdp'}, dimensions={0}, use_global_device_ids=true | all-gather | bytes 663552 | tf_op jit(solution)/shard_map/all_gather | solution.py:139
  733.9 33.8 %all-gather.8 = bf16[512,1,576]{2,0,1:T(8,128)(2,1)} all-gather(bf16[64,1,576]{2,0,1:T(8,128)(2,1)S(1)} %slice.149), channel_id=10, replica_groups=mesh['pipe'=2,'fsdp'=8,'tp'=2] {'fsdp'}, dimensions={0}, use_global_device_ids=true | all-gather | bytes 663552 | tf_op jit(solution)/shard_map/all_gather | solution.py:139
  767.6 33.6 %all_gather.123 = bf16[512,576]{1,0:T(8,128)(2,1)} all-gather(bf16[64,576]{1,0:T(8,128)(2,1)S(1)} %fusion.350), channel_id=1, replica_groups=mesh['pipe'=2,'fsdp'=8,'tp'=2] {'fsdp'}, dimensions={0}, use_global_device_ids=true | all-gather | bytes 663552 | tf_op jit(solution)/shard_map/all_gather | solution.py:140
  876.5 54.0 %reduce-scatter.59.cloned.1.call-done = f32[64,576]{1,0:T(8,128)} async-done(((f32[512,576]{1,0:T(8,128)}), f32[64,576]{1,0:T(8,128)}) %reduce-scatter.59.cloned.1.call-update) | async-done | bytes 147472 | tf_op jit(solution)/shard_map/reduce_scatter | solution.py:253
  932.0 65.9 %reduce-scatter.57.cloned.1.call-done = f32[64,576]{1,0:T(8,128)} async-done(((f32[512,576]{1,0:T(8,128)}), f32[64,576]{1,0:T(8,128)}) %reduce-scatter.57.cloned.1.call-update) | async-done | bytes 147472 | tf_op jit(solution)/shard_map/reduce_scatter | solution.py:252
  1062.9 58.1 %reduce-scatter.67.cloned.1.call-done = f32[64,576]{1,0:T(8,128)} async-done(((f32[512,576]{1,0:T(8,128)}), f32[64,576]{1,0:T(8,128)}) %reduce-scatter.67.cloned.1.call-update) | async-done | bytes 147472 | tf_op jit(solution)/shard_map/reduce_scatter | solution.py:253
  1122.5 65.7 %reduce-scatter.65.cloned.1.call-done = f32[64,576]{1,0:T(8,128)} async-done(((f32[512,576]{1,0:T(8,128)}), f32[64,576]{1,0:T(8,128)}) %reduce-scatter.65.cloned.1.call-update) | async-done | bytes 147472 | tf_op jit(solution)/shard_map/reduce_scatter | solution.py:252
  1253.6 58.1 %reduce-scatter.75.cloned.1.call-done = f32[64,576]{1,0:T(8,128)} async-done(((f32[512,576]{1,0:T(8,128)}), f32[64,576]{1,0:T(8,128)}) %reduce-scatter.75.cloned.1.call-update) | async-done | bytes 147472 | tf_op jit(solution)/shard_map/reduce_scatter | solution.py:253
  1313.2 65.7 %reduce-scatter.73.cloned.1.call-done = f32[64,576]{1,0:T(8,128)} async-done(((f32[512,576]{1,0:T(8,128)}), f32[64,576]{1,0:T(8,128)}) %reduce-scatter.73.cloned.1.call-update) | async-done | bytes 147472 | tf_op jit(solution)/shard_map/reduce_scatter | solution.py:252
  1445.1 58.1 %reduce-scatter.83.cloned.1.call-done = f32[64,576]{1,0:T(8,128)} async-done(((f32[512,576]{1,0:T(8,128)}), f32[64,576]{1,0:T(8,128)}) %reduce-scatter.83.cloned.1.call-update) | async-done | bytes 147472 | tf_op jit(solution)/shard_map/reduce_scatter | solution.py:253
  1504.8 66.0 %reduce-scatter.81.cloned.1.call-done = f32[64,576]{1,0:T(8,128)} async-done(((f32[512,576]{1,0:T(8,128)}), f32[64,576]{1,0:T(8,128)}) %reduce-scatter.81.cloned.1.call-update) | async-done | bytes 147472 | tf_op jit(solution)/shard_map/reduce_scatter | solution.py:252
  1640.3 51.5 %reduce-scatter.91.cloned.1.call-done = f32[64,576]{1,0:T(8,128)} async-done(((f32[512,576]{1,0:T(8,128)}), f32[64,576]{1,0:T(8,128)}) %reduce-scatter.91.cloned.1.call-update) | async-done | bytes 147472 | tf_op jit(solution)/shard_map/reduce_scatter | solution.py:253
  1692.8 66.6 %reduce-scatter.89.cloned.1.call-done = f32[64,576]{1,0:T(8,128)} async-done(((f32[512,576]{1,0:T(8,128)}), f32[64,576]{1,0:T(8,128)}) %reduce-scatter.89.cloned.1.call-update) | async-done | bytes 147472 | tf_op jit(solution)/shard_map/reduce_scatter | solution.py:252
  1849.6 36.4 %all-reduce.1 = (f32[1,2,576]{2,1,0:T(2,128)}, f32[1,2152]{1,0:T(1,128)}) all-reduce(f32[1,2,576]{2,1,0:T(2,128)S(1)} %fusion.503, f32[1,2152]{1,0:T(1,128)S(1)} %broadcast_in_dim.550), channel_id=1, replica_groups=mesh['pipe'=2,'fsdp'=8,'tp'=2] {'fsdp'}, use_global_device_ids=true, to_apply=%region_116.117 | all-reduce | flops 3304 | bytes 26432 | tf_op jit(solution)/shard_map/psum | solution.py:306
  1887.3 62.2 %all-reduce = (f32[1,1152]{1,0:T(1,128)}, f32[1,1152]{1,0:T(1,128)}, f32[1,1152]{1,0:T(1,128)}, f32[1,1152]{1,0:T(1,128)}, f32[1,1152]{1,0:T(1,128)}, /*index=5*/f32[1,1152]{1,0:T(1,128)}) all-reduce(f32[1,1152]{1,0:T(1,128)S(1)} %broadcast_in_dim.541, ...), channel_id=1, replica_groups=mesh['pipe'=2,'fsdp'=8,'tp'=2] {'fsdp','tp'}, use_global_device_ids=true, to_apply=%region_123.124 | all-reduce | flops 6912 | bytes 55296 | tf_op jit(solution)/shard_map/psum | solution.py:307
  1952.9 63.9 %reduce-scatter.95.cloned.1.call-done = f32[144,3,576]{2,0,1:T(8,128)} async-done(((f32[1152,3,576]{2,0,1:T(8,128)}), f32[144,3,576]{2,0,1:T(8,128)}) %reduce-scatter.95.cloned.1.call-update) | async-done | bytes 995344 | tf_op jit(solution)/shard_map/reduce_scatter | solution.py:301
  2016.8 177.1 %reduce-scatter.99.cloned.1.call-done = f32[144,2152]{1,0:T(8,128)} async-done(((f32[1152,2152]{1,0:T(8,128)}), f32[144,2152]{1,0:T(8,128)}) %reduce-scatter.99.cloned.1.call-update) | async-done | bytes 1239568 | tf_op jit(solution)/shard_map/reduce_scatter | solution.py:303
  2194.0 176.8 %reduce-scatter.101.cloned.1.call-done = f32[144,2152]{1,0:T(8,128)} async-done(((f32[1152,2152]{1,0:T(8,128)}), f32[144,2152]{1,0:T(8,128)}) %reduce-scatter.101.cloned.1.call-update) | async-done | bytes 1239568 | tf_op jit(solution)/shard_map/reduce_scatter | solution.py:304
  (1077 shorter events, 800.9 us)
Async XLA Ops:
  7.9 153.1 %all-gather.17.cloned.1.call-start = ((), (), s32[]{:S(2)}) async-start(), calls=%async_computation.69 | async-start | bytes 1658880 | tf_op jit(solution)/shard_map/all_gather | solution.py:100
  8.7 162.2 %reduce-scatter.35.cloned.1.call-start = ((), (), s32[]{:S(2)}) async-start(), calls=%async_computation.34 | async-start | bytes 442368 | tf_op jit(solution)/shard_map/reduce_scatter | solution.py:35
  163.7 93.3 %all-gather.19.cloned.1.call-start = ((), (), s32[]{:S(2)}) async-start(), calls=%async_computation.70 | async-start | bytes 5640192 | tf_op jit(solution)/shard_map/all_gather | solution.py:101
  164.3 176.1 %all-gather.21.cloned.1.call-start = ((), (), s32[]{:S(2)}) async-start(), calls=%async_computation.71 | async-start | bytes 5640192 | tf_op jit(solution)/shard_map/all_gather | solution.py:102
  164.9 186.4 %reduce-scatter.37.cloned.1.call-start = ((), (), s32[]{:S(2)}) async-start(), calls=%async_computation.35 | async-start | bytes 442368 | tf_op jit(solution)/shard_map/reduce_scatter | solution.py:35
  345.2 99.7 %reduce-scatter.39.cloned.1.call-start = ((), (), s32[]{:S(2)}) async-start(), calls=%async_computation.36 | async-start | bytes 442368 | tf_op jit(solution)/shard_map/reduce_scatter | solution.py:35
  458.1 112.2 %reduce-scatter.43.cloned.1.call-start = ((), (), s32[]{:S(2)}) async-start(), calls=%async_computation.38 | async-start | bytes 442368 | tf_op jit(solution)/shard_map/reduce_scatter | solution.py:35
  583.2 112.0 %reduce-scatter.47.cloned.1.call-start = ((), (), s32[]{:S(2)}) async-start(), calls=%async_computation.40 | async-start | bytes 442368 | tf_op jit(solution)/shard_map/reduce_scatter | solution.py:35
  708.2 115.3 %reduce-scatter.51.cloned.1.call-start = ((), (), s32[]{:S(2)}) async-start(), calls=%async_computation.42 | async-start | bytes 442368 | tf_op jit(solution)/shard_map/reduce_scatter | solution.py:35
  864.1 133.9 %reduce-scatter.57.cloned.1.call-start = ((), (), s32[]{:S(2)}) async-start(), calls=%async_computation.45 | async-start | bytes 1474560 | tf_op jit(solution)/shard_map/reduce_scatter | solution.py:252
  870.0 140.7 %reduce-scatter.61.cloned.1.call-start = ((), (), s32[]{:S(2)}) async-start(), calls=%async_computation.47 | async-start | bytes 442368 | tf_op jit(solution)/shard_map/reduce_scatter | solution.py:43
  1054.6 133.6 %reduce-scatter.65.cloned.1.call-start = ((), (), s32[]{:S(2)}) async-start(), calls=%async_computation.49 | async-start | bytes 1474560 | tf_op jit(solution)/shard_map/reduce_scatter | solution.py:252
  1060.5 140.5 %reduce-scatter.69.cloned.1.call-start = ((), (), s32[]{:S(2)}) async-start(), calls=%async_computation.51 | async-start | bytes 442368 | tf_op jit(solution)/shard_map/reduce_scatter | solution.py:43
  1245.3 133.6 %reduce-scatter.73.cloned.1.call-start = ((), (), s32[]{:S(2)}) async-start(), calls=%async_computation.53 | async-start | bytes 1474560 | tf_op jit(solution)/shard_map/reduce_scatter | solution.py:252
  1251.2 140.5 %reduce-scatter.77.cloned.1.call-start = ((), (), s32[]{:S(2)}) async-start(), calls=%async_computation.55 | async-start | bytes 442368 | tf_op jit(solution)/shard_map/reduce_scatter | solution.py:43
  1436.9 133.8 %reduce-scatter.81.cloned.1.call-start = ((), (), s32[]{:S(2)}) async-start(), calls=%async_computation.57 | async-start | bytes 1474560 | tf_op jit(solution)/shard_map/reduce_scatter | solution.py:252
  1442.8 140.7 %reduce-scatter.85.cloned.1.call-start = ((), (), s32[]{:S(2)}) async-start(), calls=%async_computation.59 | async-start | bytes 442368 | tf_op jit(solution)/shard_map/reduce_scatter | solution.py:43
  1625.6 133.8 %reduce-scatter.89.cloned.1.call-start = ((), (), s32[]{:S(2)}) async-start(), calls=%async_computation.61 | async-start | bytes 1474560 | tf_op jit(solution)/shard_map/reduce_scatter | solution.py:252
  1628.5 216.9 %reduce-scatter.53.cloned.1.call-start = ((), (), s32[]{:S(2)}) async-start(), calls=%async_computation.43 | async-start | bytes 442368 | tf_op jit(solution)/shard_map/reduce_scatter | solution.py:35
  1636.2 249.8 %reduce-scatter.93.cloned.1.call-start = ((), (), s32[]{:S(2)}) async-start(), calls=%async_computation.63 | async-start | bytes 442368 | tf_op jit(solution)/shard_map/reduce_scatter | solution.py:43
  1764.7 188.2 %reduce-scatter.97.cloned.1.call-start = ((), (), s32[]{:S(2)}) async-start(), calls=%async_computation.65 | async-start | bytes 3317760 | tf_op jit(solution)/shard_map/reduce_scatter | solution.py:302
  1769.4 247.4 %reduce-scatter.95.cloned.1.call-start = ((), (), s32[]{:S(2)}) async-start(), calls=%async_computation.64 | async-start | bytes 9953280 | tf_op jit(solution)/shard_map/reduce_scatter | solution.py:301
  1799.4 394.5 %reduce-scatter.99.cloned.1.call-start = ((), (), s32[]{:S(2)}) async-start(), calls=%async_computation.66 | async-start | bytes 11280384 | tf_op jit(solution)/shard_map/reduce_scatter | solution.py:303
  1812.3 558.5 %reduce-scatter.101.cloned.1.call-start = ((), (), s32[]{:S(2)}) async-start(), calls=%async_computation.67 | async-start | bytes 11280384 | tf_op jit(solution)/shard_map/reduce_scatter | solution.py:304
  (271 other events, 8628.3 us)
Sparse Core Ops, SparseCore 0:
  10.2 78.3 all-gather.14
  90.8 47.5 all-gather.16
  172.9 84.1 all-gather.18
  259.1 81.2 all-gather.20
  434.8 10.0 reduce-scatter.38
  458.2 8.8 reduce-scatter.40
  560.0 10.2 reduce-scatter.42
  685.1 10.0 reduce-scatter.46
  810.5 10.2 reduce-scatter.50
  839.3 10.3 reduce-scatter.54
  864.2 66.2 reduce-scatter.58
  933.7 64.1 reduce-scatter.56
  1054.7 66.1 reduce-scatter.66
  1124.2 63.9 reduce-scatter.64
  1245.4 66.2 reduce-scatter.74
  1314.9 63.9 reduce-scatter.72
  1437.0 66.1 reduce-scatter.82
  1506.6 64.0 reduce-scatter.80
  1625.7 66.1 reduce-scatter.90
  1695.3 64.0 reduce-scatter.88
  1784.0 74.3 reduce-scatter.96
  1862.5 154.3 reduce-scatter.94
  2020.9 172.9 reduce-scatter.98
  2198.2 172.5 reduce-scatter.100
  (14 shorter events, 104.8 us)
where the time goes:
time: 2390 us; the launch traced here: 2380 us
  waiting for transfers between devices  1380 us (58%)
  blocking collectives  469 us (20%)
  matrix products  249 us (10%)
  local copies, waits for them, and re-layouts  132 us (6%)
  other arithmetic  110 us (5%)
    reduce_scatter x5, waiting for transfers between devices, body(): lax.psum_scatter(key_part, 'fsdp', scatter_dimension=0, tiled=True)  330 us
    reduce_scatter x5, waiting for transfers between devices, body(): lax.psum_scatter(value_part, 'fsdp', scatter_dimension=0, tiled=True)  280 us
    reduce_scatter x1, waiting for transfers between devices, body(): lax.psum_scatter(totals[2], 'fsdp', scatter_dimension=0, tiled=True)  177 us
    reduce_scatter x1, waiting for transfers between devices, body(): lax.psum_scatter(totals[3], 'fsdp', scatter_dimension=0, tiled=True)  177 us
    all_gather x5, blocking collectives, body(): lax.all_gather(keys_own, 'fsdp', axis=0, tiled=True)  166 us
    all_gather x5, blocking collectives, body(): lax.all_gather(values_own, 'fsdp', axis=0, tiled=True)  165 us
    all_gather x1, waiting for transfers between devices, body(): lax.all_gather(up_projection[0], 'fsdp', axis=0, tiled=True)  82.8 us
    all_gather x1, waiting for transfers between devices, body(): lax.all_gather(down_projection[0], 'fsdp', axis=0, tiled=True)  77.3 us
  transfers between devices with their start and end apart: 46, of which 41 were waited for; matrix products, arithmetic and copies ran while one was open for 10% of the time, Pallas kernels for 0%

commit v1 on v0

--- a/solution.py
+++ b/solution.py
@@ -4,8 +4,6 @@
 from jax.sharding import PartitionSpec as P
 
 HD = 72
-
-
 EPSILON = 1e-06
 MASKED = -1e30
 
@@ -333,6 +331,508 @@
     )
 
 
+LANES = 128
+
+
+def swap_pairs(count, step):
+    return [(at, at ^ step) for at in range(count)]
+
+
+def pick(take_first, first, second):
+    return jnp.where(take_first, first, second)
+
+
+class Plane:
+    def __init__(self, planes):
+        self.groups = lax.axis_size("fsdp")
+        self.planes = planes
+        self.across = lax.axis_index("pipe")
+        place = lax.axis_index("fsdp")
+        self.near = self.groups // planes
+        self.plane = place // self.near
+        self.side = place % self.near
+        self.core = lax.axis_index("tp")
+
+    def pipe(self, value):
+        return lax.ppermute(value, "pipe", [(0, 1), (1, 0)])
+
+    def beside(self, value):
+        return lax.ppermute(value, "fsdp", swap_pairs(self.groups, 1))
+
+    def corner(self, value):
+        pairs = [
+            (one * self.groups + at, (1 - one) * self.groups + (at ^ 1))
+            for one in range(2)
+            for at in range(self.groups)
+        ]
+        return lax.ppermute(value, ("pipe", "fsdp"), pairs)
+
+    def core_swap(self, value):
+        return lax.ppermute(value, "tp", [(0, 1), (1, 0)])
+
+    def plane_shift(self, value, steps):
+        pairs = [(at, (at + steps * self.near) % self.groups) for at in range(self.groups)]
+        return lax.ppermute(value, "fsdp", pairs)
+
+    def plane_lists(self):
+        return [
+            [plane * self.near + side for plane in range(self.planes)] for side in range(self.near)
+        ]
+
+    def gather_rows(self, own):
+        mine = jnp.concatenate((own, self.pipe(own), self.beside(own), self.corner(own)), axis=0)
+        return jnp.concatenate((mine, self.core_swap(mine)), axis=0)
+
+    def reduce_rows(self, partial):
+        half = partial.shape[0] // 2
+        quarter = half // 4
+        low = jnp.bfloat16
+        chip = partial[:half] + self.core_swap(partial[half:].astype(low)).astype(jnp.float32)
+        low_chip = chip.astype(low)
+        return (
+            chip[:quarter]
+            + self.pipe(low_chip[quarter : 2 * quarter]).astype(jnp.float32)
+            + self.beside(low_chip[2 * quarter : 3 * quarter]).astype(jnp.float32)
+            + self.corner(low_chip[3 * quarter :]).astype(jnp.float32)
+        )
+
+    def relative(self, parts, axis_note=None):
+        p00, p01, p10, p11 = parts
+        up = self.across == 0
+        self_0, self_1 = pick(up, p00, p10), pick(up, p01, p11)
+        other_0, other_1 = pick(up, p10, p00), pick(up, p11, p01)
+        first = self.side == 0
+        return (
+            pick(first, self_0, self_1),
+            pick(first, other_0, other_1),
+            pick(first, self_1, self_0),
+            pick(first, other_1, other_0),
+        )
+
+    def absolute(self, parts):
+        one, pipe, beside, corner = parts
+        first = self.side == 0
+        self_0, self_1 = pick(first, one, beside), pick(first, beside, one)
+        other_0, other_1 = pick(first, pipe, corner), pick(first, corner, pipe)
+        up = self.across == 0
+        return (
+            pick(up, self_0, other_0),
+            pick(up, self_1, other_1),
+            pick(up, other_0, self_0),
+            pick(up, other_1, self_1),
+        )
+
+    def spread_weight(self, shard):
+        one, pipe, beside, corner = self.relative([shard[:, at] for at in range(4)])
+        pipe, beside, corner = self.pipe(pipe), self.beside(beside), self.corner(corner)
+        first = self.side == 0
+        same = jnp.concatenate((pick(first, one, beside), pick(first, beside, one)), axis=0)
+        other = jnp.concatenate((pick(first, pipe, corner), pick(first, corner, pipe)), axis=0)
+        up = self.across == 0
+        return pick(up, same, other), pick(up, other, same)
+
+    def gather_planes(self, value):
+        return lax.all_gather(
+            value, "fsdp", axis=0, tiled=True, axis_index_groups=self.plane_lists()
+        )
+
+    def reduce_planes(self, value):
+        return lax.psum_scatter(
+            value, "fsdp", scatter_dimension=0, tiled=True, axis_index_groups=self.plane_lists()
+        )
+
+    def collect_weight(self, first_section, second_section):
+        rows = first_section.shape[0] // 2
+        up = self.across == 0
+        same, other = pick(up, first_section, second_section), pick(up, second_section, first_section)
+        first = self.side == 0
+        parts = (
+            pick(first, same[:rows], same[rows:]),
+            self.pipe(pick(first, other[:rows], other[rows:])),
+            self.beside(pick(first, same[rows:], same[:rows])),
+            self.corner(pick(first, other[rows:], other[:rows])),
+        )
+        return self.absolute(parts)
+
+    def rows_in(self, value):
+        got = [lax.dynamic_index_in_dim(value, self.plane, 0, keepdims=False)]
+        for steps in range(1, self.planes):
+            target = (self.plane + steps) % self.planes
+            sent = lax.dynamic_index_in_dim(value, target, 0, keepdims=False)
+            got.append(self.plane_shift(sent, steps))
+        return self.turned(got)
+
+    def turned(self, got):
+        stacked = jnp.stack(got)
+        order = [(self.plane + self.planes - at) % self.planes for at in range(self.planes)]
+        return jnp.stack(
+            [lax.dynamic_index_in_dim(stacked, at, 0, keepdims=False) for at in order]
+        )
+
+    def halves(self, value):
+        half = self.planes // 2
+        flat = value.reshape(2, half * value.shape[1], value.shape[2])
+        up = self.across == 0
+        return pick(up, flat[0], flat[1]), pick(up, flat[1], flat[0])
+
+    def rows_out(self, first_section, second_section):
+        up = self.across == 0
+        kept = pick(up, first_section, second_section)
+        came = self.pipe(pick(up, second_section, first_section))
+        both = jnp.concatenate((pick(up, kept, came), pick(up, came, kept)), axis=0)
+        blocks = both.reshape(self.planes, both.shape[0] // self.planes, both.shape[1])
+        return self.rows_in(blocks)
+
+
+def norm_parts(values):
+    row_mean = jnp.mean(values, axis=-1, keepdims=True)
+    center = values - row_mean
+    spread = jnp.mean(center * center, axis=-1, keepdims=True)
+    scale = lax.rsqrt(spread + EPSILON)
+    return center * scale, scale
+
+
+def norm_forward(values, gain_vec, shift_vec):
+    return norm_parts(values)[0] * gain_vec + shift_vec
+
+
+def norm_backward(values, gain_vec, grad):
+    shape, scale = norm_parts(values)
+    inner = grad * gain_vec
+    mean_one = jnp.mean(inner, axis=-1, keepdims=True)
+    mean_two = jnp.mean(inner * shape, axis=-1, keepdims=True)
+    back = (inner - mean_one - shape * mean_two) * scale
+    return back, jnp.sum(grad * shape, axis=0), jnp.sum(grad, axis=0)
+
+
+def mul(left, right):
+    return jnp.dot(left, right, preferred_element_type=jnp.float32)
+
+
+def mul_first(left, right):
+    return lax.dot_general(left, right, (((0,), (0,)), ((), ())), preferred_element_type=jnp.float32)
+
+
+def pad_heads(value, parts, lanes):
+    lead = value.shape[:-1]
+    split = value.reshape(lead + (parts, HD))
+    wide = jnp.pad(split, [(0, 0)] * len(lead) + [(0, 0), (0, lanes - HD)])
+    return wide.reshape(lead + (parts * lanes,))
+
+
+def unpad_heads(value, parts, lanes):
+    return jnp.concatenate(
+        [value[..., at * lanes : at * lanes + HD] for at in range(parts)], axis=-1
+    )
+
+
+def gelu_both(values):
+    root = (2.0 / jnp.pi) ** 0.5
+    square = values * values
+    inside = jnp.tanh(root * values * (1.0 + 0.044715 * square))
+    value = 0.5 * values * (1.0 + inside)
+    slope = 0.5 * (1.0 + inside) + 0.5 * values * (1.0 - inside * inside) * root * (
+        1.0 + 3.0 * 0.044715 * square
+    )
+    return value, slope
+
+
+def attend(query, keys, values, same_image):
+    scores = contract_last(query, keys) * HD ** (-0.5)
+    scores = jnp.where(same_image, scores, MASKED)
+    row_max = jnp.max(scores, axis=-1, keepdims=True)
+    exp_scores = jnp.exp(scores - row_max)
+    probs = exp_scores / jnp.sum(exp_scores, axis=-1, keepdims=True)
+    return mul(probs.astype(jnp.bfloat16), values), probs
+
+
+def attend_back(query, keys, values, probs, context_grad):
+    prob_grad = contract_last(context_grad, values)
+    inner = jnp.sum(probs * prob_grad, axis=-1, keepdims=True)
+    score_grad = (probs * (prob_grad - inner)).astype(jnp.bfloat16)
+    scale = HD ** (-0.5)
+    return (
+        mul(score_grad, keys) * scale,
+        mul_first(score_grad, query) * scale,
+        mul_first(probs.astype(jnp.bfloat16), context_grad),
+    )
+
+
+class Section:
+    def __init__(self, plane, heads, weights, vectors):
+        self.plane = plane
+        self.heads = heads
+        into, out, self.up, self.down = weights
+        self.into = pad_heads(into, 3 * heads, LANES)
+        self.out = pad_heads(out, heads, LANES)
+        (
+            self.query_bias,
+            self.value_bias,
+            self.up_bias,
+            self.out_bias,
+            self.gain_attn,
+            self.shift_attn,
+            self.down_bias,
+            self.gain_feed,
+            self.shift_feed,
+        ) = vectors
+
+    def norm_attn(self, rows):
+        return norm_forward(rows, self.gain_attn, self.shift_attn).astype(jnp.bfloat16)
+
+    def head(self, value, at):
+        return value[:, at * LANES : (at + 1) * LANES]
+
+    def forward(self, rows, normed, same_image, last):
+        plane, heads = self.plane, self.heads
+        width = heads * LANES
+        self.rows, self.normed, self.same_image = rows, normed, same_image
+        projected = mul(normed, self.into)
+        self.query = (projected[:, :width] + self.query_bias).astype(jnp.bfloat16)
+        self.keys = projected[:, width : 2 * width].astype(jnp.bfloat16)
+        self.values = (projected[:, 2 * width :] + self.value_bias).astype(jnp.bfloat16)
+        context, self.probs = [], []
+        for at in range(heads):
+            one, probs = attend(
+                self.head(self.query, at), self.head(self.keys, at), self.head(self.values, at), same_image
+            )
+            context.append(one.astype(jnp.bfloat16))
+            self.probs.append(probs)
+        self.context = jnp.concatenate(context, axis=1)
+        self.middle = rows + plane.reduce_rows(contract_last(self.context, self.out)) + self.out_bias
+        feed = norm_forward(self.middle, self.gain_feed, self.shift_feed).astype(jnp.bfloat16)
+        self.feed = plane.gather_rows(feed)
+        self.hidden = mul(self.feed, self.up) + self.up_bias
+        self.active = gelu_both(self.hidden)[0].astype(jnp.bfloat16)
+        fed = plane.reduce_rows(contract_last(self.active, self.down))
+        return (self.middle + fed + self.down_bias).astype(jnp.bfloat16)
+
+    def backward(self, grad, gathered):
+        plane, heads = self.plane, self.heads
+        low = jnp.bfloat16
+        grad_down = mul_first(gathered, self.active).astype(low)
+        active_grad = mul(gathered, self.down)
+        hidden_grad = (active_grad * gelu_both(self.hidden)[1]).astype(low)
+        feed_grad = plane.reduce_rows(contract_last(hidden_grad, self.up))
+        grad_up = mul_first(self.feed, hidden_grad).astype(low)
+        grad_up_bias = jnp.sum(hidden_grad.astype(jnp.float32), axis=0)
+        back, grad_gain_feed, grad_shift_feed = norm_backward(self.middle, self.gain_feed, feed_grad)
+        middle_grad = grad + back
+        attn_grad = plane.gather_rows(middle_grad.astype(low))
+        context_grad = mul(attn_grad, self.out).astype(low)
+        grad_out = mul_first(attn_grad, self.context)
+        grads = [[], [], []]
+        for at in range(heads):
+            parts = attend_back(
+                self.head(self.query, at),
+                self.head(self.keys, at),
+                self.head(self.values, at),
+                self.probs[at],
+                self.head(context_grad, at),
+            )
+            for kept, part in zip(grads, parts):
+                kept.append(part.astype(low))
+        joined = jnp.concatenate(grads[0] + grads[1] + grads[2], axis=1)
+        normed_grad = plane.reduce_rows(contract_last(joined, self.into))
+        grad_in = mul_first(self.normed, joined)
+        wide_sums = jnp.sum(joined.astype(jnp.float32), axis=0)
+        rows_back, grad_gain_attn, grad_shift_attn = norm_backward(self.rows, self.gain_attn, normed_grad)
+        result = (middle_grad + rows_back).astype(low)
+        weights = (
+            unpad_heads(grad_in.astype(low), 3 * heads, LANES),
+            unpad_heads(grad_out.astype(low), heads, LANES),
+            grad_up,
+            grad_down,
+        )
+        sums = (
+            jnp.sum(middle_grad, axis=0),
+            grad_gain_attn,
+            grad_shift_attn,
+            jnp.sum(grad, axis=0),
+            grad_gain_feed,
+            grad_shift_feed,
+        )
+        bias_sums = unpad_heads(wide_sums, 3 * heads, LANES)
+        own = heads * HD
+        columns = jnp.concatenate((bias_sums[:own], bias_sums[2 * own :], grad_up_bias))
+        return result, weights, sums, columns
+
+
+def plane_body(
+    inputs,
+    cotangent,
+    image_ids,
+    proj_in,
+    bias_in,
+    proj_out,
+    bias_out,
+    gain_attn,
+    shift_attn,
+    up_projection,
+    up_bias_vector,
+    down_projection,
+    bias_down,
+    gain_feed,
+    shift_feed,
+):
+    micro_count, part_rows, model_width = inputs.shape
+    local_cols = proj_in.shape[3]
+    hidden_cols = up_projection.shape[2]
+    shard_rows = proj_in.shape[1]
+    plane = Plane(micro_count)
+    shares = 4
+    own_cols = local_cols // shares
+    own_hidden = hidden_cols // shares
+    heads = own_cols // HD
+    up = plane.across == 0
+    share_num = plane.across * 2 + plane.side
+
+    rows_all = plane.rows_in(inputs)
+
+    tail = -hidden_cols % model_width
+    vec = jnp.concatenate(
+        [bias_in[0].reshape(-1), bias_out[0], gain_attn[0], shift_attn[0], bias_down[0], gain_feed[0], shift_feed[0]]
+        + [up_bias_vector[0], jnp.zeros((tail,), jnp.bfloat16)]
+    ).reshape(-1, model_width)
+    vec_other = plane.pipe(vec)
+
+    def vectors(section):
+        chosen = pick(up == (section == 0), vec, vec_other).astype(jnp.float32)
+        query_all = chosen[0, :local_cols].reshape(shares, own_cols)
+        value_all = chosen[0, local_cols:].reshape(shares, own_cols)
+        hidden_all = chosen[7:].reshape(-1)[:hidden_cols].reshape(shares, own_hidden)
+        mine = [
+            lax.dynamic_index_in_dim(one, share_num, 0, keepdims=False)
+            for one in (query_all, value_all, hidden_all)
+        ]
+        wide = [pad_heads(one, heads, LANES) for one in mine[:2]]
+        return (wide[0], wide[1], mine[2]) + tuple(chosen[at] for at in range(1, 7))
+
+    split_in = jnp.swapaxes(proj_in[0].reshape(shard_rows, 3, shares, own_cols), 1, 2).reshape(
+        shard_rows, shares, 3 * own_cols
+    )
+    shards = (
+        split_in,
+        proj_out[0].reshape(shard_rows, shares, own_cols),
+        up_projection[0].reshape(shard_rows, shares, own_hidden),
+        down_projection[0].reshape(shard_rows, shares, own_hidden),
+    )
+    spread = [plane.spread_weight(shard) for shard in shards]
+    whole = [[plane.gather_planes(pair[section]) for pair in spread] for section in range(2)]
+    sections = [Section(plane, heads, whole[section], vectors(section)) for section in range(2)]
+
+    ids = lax.dynamic_index_in_dim(image_ids, plane.plane, 0, keepdims=False)
+    ids = ids.reshape(2, micro_count // 2, 2, 2, part_rows)
+    ids = pick(up, ids, jnp.flip(ids, 0))
+    ids = pick(plane.side == 0, ids, jnp.flip(ids, 2))
+    ids = pick(plane.core == 0, ids, jnp.flip(ids, 3))
+    ids = ids.transpose(3, 2, 0, 1, 4).reshape(-1)
+    same_image = ids[:, None] == ids[None, :]
+
+    own_rows, pair_rows = plane.halves(rows_all)
+    first = sections[0]
+    pair_normed = first.norm_attn(jnp.concatenate((own_rows, pair_rows), axis=0).astype(jnp.float32))
+    mine = jnp.concatenate((pair_normed, plane.beside(pair_normed)), axis=0)
+    normed = jnp.concatenate((mine, plane.core_swap(mine)), axis=0)
+    result = []
+    rows = own_rows
+    for section in range(2):
+        one = sections[section]
+        rows = rows.astype(jnp.float32)
+        if section > 0:
+            normed = plane.gather_rows(one.norm_attn(rows))
+        rows = one.forward(rows, normed, same_image, section == 1)
+        result.append(rows)
+
+    given = plane.rows_in(cotangent)
+    own_given, pair_given = plane.halves(given)
+    pair = jnp.concatenate((own_given, pair_given), axis=0)
+    mine = jnp.concatenate((pair, plane.beside(pair)), axis=0)
+    gathered = jnp.concatenate((mine, plane.core_swap(mine)), axis=0)
+    grad = own_given
+    back = [None, None]
+    weight_grads, sums, columns = [None, None], [None, None], [None, None]
+    for section in (1, 0):
+        if section == 0:
+            gathered = plane.gather_rows(grad)
+        grad, weights, sums[section], columns[section] = sections[section].backward(
+            grad.astype(jnp.float32), gathered
+        )
+        back[section] = grad
+        weight_grads[section] = [plane.reduce_planes(one) for one in weights]
+
+    activations = plane.rows_out(result[0], result[1])
+    grad_inputs = plane.rows_out(back[0], back[1])
+    blocks = [
+        plane.collect_weight(one, two) for one, two in zip(weight_grads[0], weight_grads[1])
+    ]
+    blocks = [[part.astype(jnp.float32) for part in four] for four in blocks]
+    grad_in = jnp.concatenate(
+        [part.reshape(shard_rows, 3, own_cols) for part in blocks[0]], axis=2
+    )
+    grad_out, grad_up, grad_down = [jnp.concatenate(four, axis=1) for four in blocks[1:]]
+
+    column_count = columns[0].shape[0]
+    pad = -column_count % model_width
+    packs = [
+        jnp.concatenate(sums[section] + (columns[section], jnp.zeros((pad,), jnp.float32))).reshape(-1, model_width)
+        for section in range(2)
+    ]
+    pack = jnp.concatenate(packs, axis=0)
+    both = pack + plane.core_swap(pack)
+    per = packs[0].shape[0]
+    rolled = jnp.stack([both[:6], both[per : per + 6]])
+    held = jnp.stack([pack[6:per], pack[per + 6 :]])
+    message = jnp.concatenate((rolled, held), axis=1)
+    send_same = pick(up, message[0], message[1])
+    send_other = pick(up, message[1], message[0])
+    parts = (send_same, plane.pipe(send_other), plane.beside(send_same), plane.corner(send_other))
+    ordered = plane.absolute(parts)
+    total = parts[0][:6] + parts[1][:6] + parts[2][:6] + parts[3][:6]
+    kept = jnp.concatenate([total] + [part[6:] for part in ordered], axis=0)
+    full = kept
+    for steps in range(1, plane.planes):
+        full = full + plane.plane_shift(kept, steps)
+    parts = full[6:].reshape(shares, -1)[:, :column_count]
+    grad_bias_in = jnp.stack(
+        (parts[:, :own_cols].reshape(-1), parts[:, own_cols : 2 * own_cols].reshape(-1))
+    )
+    grad_up_bias = parts[:, 2 * own_cols :].reshape(-1)
+    return (
+        activations[None],
+        grad_inputs[None],
+        grad_in[None],
+        grad_bias_in[None],
+        grad_out[None],
+        full[0][None],
+        full[1][None],
+        full[2][None],
+        grad_up[None],
+        grad_up_bias[None],
+        grad_down[None],
+        full[3][None],
+        full[4][None],
+        full[5][None],
+    )
+
+
+def fits_planes(inputs, proj_in, up_projection):
+    micro_count = inputs.shape[0]
+    return (
+        lax.axis_size("pipe") == 2
+        and lax.axis_size("tp") == 2
+        and micro_count % 2 == 0
+        and lax.axis_size("fsdp") == 2 * micro_count
+        and proj_in.shape[3] % (4 * HD) == 0
+        and up_projection.shape[2] % 4 == 0
+    )
+
+
+def choose(inputs, cotangent, image_ids, proj_in, *rest):
+    form = plane_body if fits_planes(inputs, proj_in, rest[5]) else body
+    return form(inputs, cotangent, image_ids, proj_in, *rest)
+
+
 def solution(mesh):
     placed = (
         P(None, ("fsdp", "tp"), None),
@@ -352,7 +852,7 @@
         P("pipe", None),
     )
     return jax.shard_map(
-        body,
+        choose,
         mesh=mesh,
         in_specs=placed,
         out_specs=(

time: 2390 us -> 706 us (0.30)
  waiting for transfers between devices: 1380 us -> 293 us
  blocking collectives: 469 us -> 76.2 us
  matrix products: 249 us -> 63.1 us
  starting transfers between devices: 22.3 us -> 123 us
  local copies, waits for them, and re-layouts: 132 us -> 73.1 us
  other arithmetic: 110 us -> 51.2 us
    reduce_scatter x34 -> x4, waiting for transfers between devices: 1120 us -> 69.3 us  [reduce_planes(): lax.psum_scatter(value, 'fsdp', scatter_dimension=0, tiled=True, axis_ind...]
    all_gather x30 -> x4, blocking collectives: 371 us -> 76.2 us  [gather_planes(): lax.all_gather(value, 'fsdp', axis=0, tiled=True, axis_index_groups=self....]
    dot_general x80 -> x32, matrix products: 206 us -> 44.4 us  [the longest x16 22.7 us: mul(): return jnp.dot(left, right, preferred_element_type=jnp.float32)]
    all_gather x4, waiting for transfers between devices: 229 us -> 75.4 us  [gather_planes(): lax.all_gather(value, 'fsdp', axis=0, tiled=True, axis_index_groups=self....]
    ppermute x8 -> x106, waiting for transfers between devices: 23.9 us -> 141 us  [the longest x25 53 us: beside(): return lax.ppermute(value, 'fsdp', swap_pairs(self.groups, 1))]
    ppermute x8 -> x106, starting transfers between devices: 19.5 us -> 122 us  [the longest x23 33.1 us: corner(): return lax.ppermute(value, ('pipe', 'fsdp'), pairs)]
    psum x2 -> x0, blocking collectives: 98.6 us -> none  [the longest x1 62.2 us: body(): lax.psum((vector_totals[0], vector_totals[1], vector_totals[2], vector_to...]
    reduce_sum x59 -> x24, other arithmetic: 50.3 us -> 11.6 us  [the longest x5 3.31 us: norm_parts(): row_mean = jnp.mean(values, axis=-1, keepdims=True)]
  transfers between devices with their start and end apart: 46 -> 118, of which waited for: 41 -> 69; matrix products, arithmetic and copies ran while one was open for 10% -> 21% of each run, Pallas kernels for 0% -> 0%
where the time goes in v1:
time: 706 us; the launch traced here: 697 us
  waiting for transfers between devices  293 us (42%)
  starting transfers between devices  123 us (17%)
  blocking collectives  76.2 us (11%)
  local copies, waits for them, and re-layouts  73.1 us (10%)
  matrix products  63.1 us (9%)
  other arithmetic  51.2 us (7%)
  between operations  17.5 us (2%)
    all_gather x4, blocking collectives, gather_planes(): lax.all_gather(value, 'fsdp', axis=0, tiled=True, axis_index_groups=self....  76.2 us
    all_gather x4, waiting for transfers between devices, gather_planes(): lax.all_gather(value, 'fsdp', axis=0, tiled=True, axis_index_groups=self....  75.4 us
    reduce_scatter x4, waiting for transfers between devices, reduce_planes(): lax.psum_scatter(value, 'fsdp', scatter_dimension=0, tiled=True, axis_ind...  69.3 us
    ppermute x25, waiting for transfers between devices, beside(): return lax.ppermute(value, 'fsdp', swap_pairs(self.groups, 1))  53 us
    unnamed x362, local copies, waits for them, and re-layouts  38.2 us
    ppermute x23, starting transfers between devices, corner(): return lax.ppermute(value, ('pipe', 'fsdp'), pairs)  33.1 us
    ppermute x26, waiting for transfers between devices, pipe(): return lax.ppermute(value, 'pipe', [(0, 1), (1, 0)])  33 us
    ppermute x25, starting transfers between devices, beside(): return lax.ppermute(value, 'fsdp', swap_pairs(self.groups, 1))  29.8 us
  transfers between devices with their start and end apart: 118, of which 69 were waited for; matrix products, arithmetic and copies ran while one was open for 21% of the time, Pallas kernels for 0%

profile of v1, /device:TPU:0, one launch (start us, length us, event | category | flops | bytes accessed | tf_op | source)
XLA Modules:
  0.0 697.3 jit_solution(1827670646774928593)
XLA Ops:
  12.4 3.9 collective-permute-start.22
  43.4 14.4 %all-gather = bf16[4,288,144]{1,2,0:T(8,128)(2,1)S(1)} all-gather(bf16[1,288,144]{1,2,0:T(8,128)(2,1)S(1)} %get-tuple-element.311), channel_id=1, replica_groups={{0,4,8,12},{2,6,10,14},{1,5,9,13},{3,7,11,15},{16,20,24,28},{18,22,26,3..., dimensions={0}, use_global_device_ids=true | all-gather | bytes 414720 | tf_op jit(solution)/shard_map/all_gather | solution.py:435
  62.5 8.5 %collective-permute-done.6 = bf16[144,432]{0,1:T(8,128)(2,1)S(1)} collective-permute-done((bf16[144,432]{0,1:T(8,128)(2,1)S(1)}, bf16[144,432]{0,1:T(8,128)(2,1)S(1)}, u32[]{:S(2)}, u32[]{:S(2)}) %collective-permute-start.6) | collective-permute-done | bytes 124448 | tf_op jit(solution)/shard_map/ppermute | solution.py:360
  73.0 4.8 collective-permute-done.8
  80.6 4.0 collective-permute-done.4
  85.5 25.0 %all_gather.24 = bf16[1152,432]{1,0:T(8,128)(2,1)S(1)} all-gather(bf16[288,432]{1,0:T(8,128)(2,1)S(1)} %copy.95), channel_id=1, replica_groups={{0,4,8,12},{2,6,10,14},{1,5,9,13},{3,7,11,15},{16,20,24,28},{18,22,26,3..., dimensions={0}, use_global_device_ids=true | all-gather | bytes 1244160 | tf_op jit(solution)/shard_map/all_gather | solution.py:435
  154.6 4.4 all-gather.7.cloned.1.call-done
  161.3 34.1 %all-gather.9.cloned.1.call-done = bf16[1152,538]{1,0:T(8,128)(2,1)} async-done(((bf16[288,538]{1,0:T(8,128)(2,1)}), bf16[1152,538]{1,0:T(8,128)(2,1)}) %all-gather.9.cloned.1.call-update) | async-done | bytes 1239568 | tf_op jit(solution)/shard_map/all_gather | solution.py:435
  195.4 4.2 fusion.156
  211.2 15.0 %all-gather.1 = bf16[4,288,144]{1,2,0:T(8,128)(2,1)S(1)} all-gather(bf16[1,288,144]{1,2,0:T(8,128)(2,1)S(1)} %copy-done.44), channel_id=1, replica_groups={{0,4,8,12},{2,6,10,14},{1,5,9,13},{3,7,11,15},{16,20,24,28},{18,22,26,3..., dimensions={0}, use_global_device_ids=true | all-gather | bytes 414720 | tf_op jit(solution)/shard_map/all_gather | solution.py:435
  232.5 21.9 %all_gather.28 = bf16[1152,432]{1,0:T(8,128)(2,1)S(1)} all-gather(bf16[288,432]{1,0:T(8,128)(2,1)S(1)} %copy.107), channel_id=1, replica_groups={{0,4,8,12},{2,6,10,14},{1,5,9,13},{3,7,11,15},{16,20,24,28},{18,22,26,3..., dimensions={0}, use_global_device_ids=true | all-gather | bytes 1244160 | tf_op jit(solution)/shard_map/all_gather | solution.py:435
  278.9 4.9 collective-permute-done.36
  298.4 4.2 all-gather.11.cloned.1.call-done
  306.3 32.6 %all-gather.13.cloned.1.call-done = bf16[1152,538]{1,0:T(8,128)(2,1)} async-done(((bf16[288,538]{1,0:T(8,128)(2,1)}), bf16[1152,538]{1,0:T(8,128)(2,1)}) %all-gather.13.cloned.1.call-update) | async-done | bytes 1239568 | tf_op jit(solution)/shard_map/all_gather | solution.py:435
  339.0 4.0 convert_reduce_fusion.2
  447.0 4.6 fusion.157
  483.6 4.3 collective-permute-done.48
  541.7 4.2 collective-permute-start.94
  551.3 5.2 collective-permute-done.95
  558.4 6.3 collective-permute-start.84
  572.6 34.2 %reduce-scatter.21.cloned.1.call-done = bf16[288,538]{1,0:T(8,128)(2,1)} async-done(((bf16[1152,538]{1,0:T(8,128)(2,1)}), bf16[288,538]{1,0:T(8,128)(2,1)}) %reduce-scatter.21.cloned.1.call-update) | async-done | bytes 309904 | tf_op jit(solution)/shard_map/reduce_scatter | solution.py:440
  606.8 35.1 %reduce-scatter.17.cloned.1.call-done = bf16[288,538]{1,0:T(8,128)(2,1)} async-done(((bf16[1152,538]{1,0:T(8,128)(2,1)}), bf16[288,538]{1,0:T(8,128)(2,1)}) %reduce-scatter.17.cloned.1.call-update) | async-done | bytes 309904 | tf_op jit(solution)/shard_map/reduce_scatter | solution.py:440
  665.6 7.2 %reduce-scatter.25.cloned.1.call-done = bf16[288,432]{1,0:T(8,128)(2,1)} async-done(((bf16[1152,432]{1,0:T(8,128)(2,1)}), bf16[288,432]{1,0:T(8,128)(2,1)}) %reduce-scatter.25.cloned.1.call-update) | async-done | bytes 248848
  682.5 4.2 collective-permute-done.89
  (898 shorter events, 388.7 us)
Async XLA Ops:
  7.2 151.7 %all-gather.7.cloned.1.call-start = ((), (), s32[]{:S(2)}) async-start(), calls=%async_computation.8 | async-start | bytes 1843200 | tf_op jit(solution)/shard_map/all_gather | solution.py:435
  12.4 99.2 %collective-permute-start.22 = (bf16[144,538]{1,0:T(8,128)(2,1)}, bf16[144,538]{1,0:T(8,128)(2,1)}, u32[]{:S(2)}, u32[]{:S(2)}) collective-permute-start(bf16[144,538]{1,0:T(8,128)(2,1)} %select_bitcast_fusion.6), channel_id=1, source_target_pairs={{0,18},{2,16},{4,22},{6,20},{8,26},{10,24},{12,30},{14,28},{16,2},... | collective-permute-start | bytes 464840 | tf_op jit(solution)/shard_map/ppermute | solution.py:368
  16.3 95.3 %collective-permute-start.21 = (bf16[144,538]{1,0:T(8,128)(2,1)}, bf16[144,538]{1,0:T(8,128)(2,1)}, u32[]{:S(2)}, u32[]{:S(2)}) collective-permute-start(bf16[144,538]{1,0:T(8,128)(2,1)} %get-tuple-element.196), channel_id=1, source_target_pairs={{0,16},{16,0},{1,17},{17,1},{2,18},{18,2},{3,19},{19,3},{4,20},{20... | collective-permute-start | bytes 464840 | tf_op jit(solution)/shard_map/ppermute | solution.py:357
  16.9 41.5 %collective-permute-start = (bf16[32,1152]{1,0:T(8,128)(2,1)S(1)}, bf16[32,1152]{1,0:T(8,128)(2,1)S(1)}, u32[]{:S(2)}, u32[]{:S(2)}) collective-permute-start(bf16[32,1152]{1,0:T(8,128)(2,1)S(1)} %get-tuple-element.317), channel_id=1, source_target_pairs={{0,4},{2,6},{4,8},{6,10},{8,12},{10,14},{12,0},{14,2},{1,5},{3,7},... | collective-permute-start | bytes 221192 | tf_op jit(solution)/shard_map/ppermute | solution.py:375
  34.4 25.6 %collective-permute-start.1 = (bf16[32,1152]{1,0:T(8,128)(2,1)S(1)}, bf16[32,1152]{1,0:T(8,128)(2,1)S(1)}, u32[]{:S(2)}, u32[]{:S(2)}) collective-permute-start(bf16[32,1152]{1,0:T(8,128)(2,1)S(1)} %get-tuple-element.319), channel_id=1, source_target_pairs={{0,8},{2,10},{4,12},{6,14},{8,0},{10,2},{12,4},{14,6},{1,9},{3,11}... | collective-permute-start | bytes 221192 | tf_op jit(solution)/shard_map/ppermute | solution.py:375
  58.4 54.8 %collective-permute-start.20 = (bf16[144,538]{1,0:T(8,128)(2,1)}, bf16[144,538]{1,0:T(8,128)(2,1)}, u32[]{:S(2)}, u32[]{:S(2)}) collective-permute-start(bf16[144,538]{1,0:T(8,128)(2,1)} %get-tuple-element.168), channel_id=1, source_target_pairs={{0,2},{2,0},{4,6},{6,4},{8,10},{10,8},{12,14},{14,12},{1,3},{3,1},... | collective-permute-start | bytes 464840 | tf_op jit(solution)/shard_map/ppermute | solution.py:360
  72.5 53.4 %collective-permute-start.23 = (bf16[144,538]{1,0:T(8,128)(2,1)}, bf16[144,538]{1,0:T(8,128)(2,1)}, u32[]{:S(2)}, u32[]{:S(2)}) collective-permute-start(bf16[144,538]{1,0:T(8,128)(2,1)} %get-tuple-element.178), channel_id=1, source_target_pairs={{0,2},{2,0},{4,6},{6,4},{8,10},{10,8},{12,14},{14,12},{1,3},{3,1},... | collective-permute-start | bytes 464840 | tf_op jit(solution)/shard_map/ppermute | solution.py:360
  85.5 28.7 %collective-permute-start.5 = (bf16[256,1152]{1,0:T(8,128)(2,1)}, bf16[256,1152]{1,0:T(8,128)(2,1)}, u32[]{:S(2)}, u32[]{:S(2)}) collective-permute-start(bf16[256,1152]{1,0:T(8,128)(2,1)} %pad_maximum_fusion.2), channel_id=1, source_target_pairs={{0,1},{1,0},{2,3},{3,2},{4,5},{5,4},{6,7},{7,6},{8,9},{9,8},{10,11... | collective-permute-start | bytes 1769480 | tf_op jit(solution)/shard_map/ppermute | solution.py:371
  122.4 73.0 %all-gather.9.cloned.1.call-start = ((), (), s32[]{:S(2)}) async-start(), calls=%async_computation.9 | async-start | bytes 1843200 | tf_op jit(solution)/shard_map/all_gather | solution.py:435
  136.4 166.2 %all-gather.11.cloned.1.call-start = ((), (), s32[]{:S(2)}) async-start(), calls=%async_computation.10 | async-start | bytes 1843200 | tf_op jit(solution)/shard_map/all_gather | solution.py:435
  201.8 66.1 %collective-permute-start.50 = (bf16[32,1152]{1,0:T(8,128)(2,1)}, bf16[32,1152]{1,0:T(8,128)(2,1)}, u32[]{:S(2)}, u32[]{:S(2)}) collective-permute-start(bf16[32,1152]{1,0:T(8,128)(2,1)} %get-tuple-element.299), channel_id=1, source_target_pairs={{0,4},{2,6},{4,8},{6,10},{8,12},{10,14},{12,0},{14,2},{1,5},{3,7},... | collective-permute-start | bytes 221192 | tf_op jit(solution)/shard_map/ppermute | solution.py:375
  202.5 65.4 %collective-permute-start.51 = (bf16[32,1152]{1,0:T(8,128)(2,1)}, bf16[32,1152]{1,0:T(8,128)(2,1)}, u32[]{:S(2)}, u32[]{:S(2)}) collective-permute-start(bf16[32,1152]{1,0:T(8,128)(2,1)} %get-tuple-element.301), channel_id=1, source_target_pairs={{0,8},{2,10},{4,12},{6,14},{8,0},{10,2},{12,4},{14,6},{1,9},{3,11}... | collective-permute-start | bytes 221192 | tf_op jit(solution)/shard_map/ppermute | solution.py:375
  229.0 26.5 %collective-permute-start.30 = (bf16[64,1152]{1,0:T(8,128)(2,1)S(1)}, bf16[64,1152]{1,0:T(8,128)(2,1)S(1)}, u32[]{:S(2)}, u32[]{:S(2)}) collective-permute-start(bf16[64,1152]{1,0:T(8,128)(2,1)S(1)} %get-tuple-element.163), channel_id=1, source_target_pairs={{0,16},{16,0},{1,17},{17,1},{2,18},{18,2},{3,19},{19,3},{4,20},{20... | collective-permute-start | bytes 442376 | tf_op jit(solution)/shard_map/ppermute | solution.py:357
  230.6 27.7 %collective-permute-start.31 = (bf16[64,1152]{1,0:T(8,128)(2,1)S(1)}, bf16[64,1152]{1,0:T(8,128)(2,1)S(1)}, u32[]{:S(2)}, u32[]{:S(2)}) collective-permute-start(bf16[64,1152]{1,0:T(8,128)(2,1)S(1)} %get-tuple-element.163), channel_id=1, source_target_pairs={{0,2},{2,0},{4,6},{6,4},{8,10},{10,8},{12,14},{14,12},{1,3},{3,1},... | collective-permute-start | bytes 442376 | tf_op jit(solution)/shard_map/ppermute | solution.py:360
  232.0 26.3 %collective-permute-start.32 = (bf16[64,1152]{1,0:T(8,128)(2,1)S(1)}, bf16[64,1152]{1,0:T(8,128)(2,1)}, u32[]{:S(2)}, u32[]{:S(2)}) collective-permute-start(bf16[64,1152]{1,0:T(8,128)(2,1)S(1)} %get-tuple-element.163), channel_id=1, source_target_pairs={{0,18},{2,16},{4,22},{6,20},{8,26},{10,24},{12,30},{14,28},{16,2},... | collective-permute-start | bytes 442376 | tf_op jit(solution)/shard_map/ppermute | solution.py:368
  268.9 70.1 %all-gather.13.cloned.1.call-start = ((), (), s32[]{:S(2)}) async-start(), calls=%async_computation.11 | async-start | bytes 1843200 | tf_op jit(solution)/shard_map/all_gather | solution.py:435
  277.6 212.1 %reduce-scatter.31.cloned.1.call-start = ((), (), s32[]{:S(2)}) async-start(), calls=%async_computation.19 | async-start | bytes 737280
  384.6 109.9 %reduce-scatter.27.cloned.1.call-start = ((), (), s32[]{:S(2)}) async-start(), calls=%async_computation.17 | async-start | bytes 1474560
  437.4 79.2 %reduce-scatter.29.cloned.1.call-start = ((), (), s32[]{:S(2)}) async-start(), calls=%async_computation.18 | async-start | bytes 737280
  443.0 129.6 %reduce-scatter.23.cloned.1.call-start = ((), (), s32[]{:S(2)}) async-start(), calls=%async_computation.15 | async-start | bytes 1843200 | tf_op jit(solution)/shard_map/reduce_scatter | solution.py:440
  446.9 125.7 %reduce-scatter.19.cloned.1.call-start = ((), (), s32[]{:S(2)}) async-start(), calls=%async_computation.13 | async-start | bytes 1843200 | tf_op jit(solution)/shard_map/reduce_scatter | solution.py:440
  457.5 149.3 %reduce-scatter.21.cloned.1.call-start = ((), (), s32[]{:S(2)}) async-start(), calls=%async_computation.14 | async-start | bytes 1843200 | tf_op jit(solution)/shard_map/reduce_scatter | solution.py:440
  473.1 168.8 %reduce-scatter.17.cloned.1.call-start = ((), (), s32[]{:S(2)}) async-start(), calls=%async_computation.12 | async-start | bytes 1843200 | tf_op jit(solution)/shard_map/reduce_scatter | solution.py:440
  494.4 178.3 %reduce-scatter.25.cloned.1.call-start = ((), (), s32[]{:S(2)}) async-start(), calls=%async_computation.16 | async-start | bytes 1474560
  (255 other events, 1680.2 us)
Sparse Core Ops, SparseCore 0:
  122.5 36.3 all-gather.6
  161.1 34.2 all-gather.8
  269.0 33.6 all-gather.10
  304.6 34.2 all-gather.12
  384.8 20.3 reduce-scatter.30
  437.5 27.5 reduce-scatter.26
  467.4 23.3 reduce-scatter.28
  493.1 33.7 reduce-scatter.22
  529.2 38.1 reduce-scatter.18
  569.6 37.2 reduce-scatter.20
  609.1 32.7 reduce-scatter.16
  644.6 28.0 reduce-scatter.24
